TPU v7x, 128 devices: a whole 4x4x4 slice. The times are simulated.
128 devices in a mesh: dp: 4 (over y), seq: 32 (over z, x, core).
Axes of the slice: x: 4, y: 4, z: 4, core: 2. Of those that a mesh axis runs over, the one named last changes fastest.
Arguments:
- queries: bfloat16 [4, 8192, 1024], P('dp', 'seq'), may hold values from -7.5 to 7.5
- keys: bfloat16 [4, 8192, 1024], P('dp', 'seq'), may hold values from -7.5 to 7.5
- values: bfloat16 [4, 8192, 1024], P('dp', 'seq'), may hold values from -7.5 to 7.5
- grad_out: bfloat16 [4, 8192, 1024], P('dp', 'seq'), may hold values from -3 to 3
- w_out: bfloat16 [1024, 1024], replicated, may hold values from -0.1875 to 0.1875
Outputs:
- mixed: bfloat16 [4, 8192, 1024], P('dp', 'seq')
- grad_queries: bfloat16 [4, 8192, 1024], P('dp', 'seq')
- grad_keys: bfloat16 [4, 8192, 1024], P('dp', 'seq')
- grad_values: bfloat16 [4, 8192, 1024], P('dp', 'seq')
- grad_w_out: float32 [1024, 1024], P(('dp', 'seq'))
All inputs are finite; a program needn't handle non-finite values.
Results may differ from a plain program's by a relative error of at most 0.03.
Values may be sent and summed in bfloat16 or wider, within the bound.
A program may use at most 128 MiB of HBM per device.

v0:
```python
import math
import jax
import jax.numpy as jnp
from jax import lax
from jax.sharding import PartitionSpec as P

HEADS = 8
HEAD_DIM = 128
BLOCK = 128
LOCAL_LEVELS = 1
LOG_TWO = math.log(2.0)


def partner(block, axis, distance):
    count = lax.axis_size(axis)
    route = []
    for low in range(count):
        high = low | 1 << distance
        if high != low and high < count:
            route += [(low, high), (high, low)]
    return lax.ppermute(block, axis, route)


def pooled(rows):
    shape = rows.shape
    pairs = rows.astype(jnp.float32).reshape(shape[:-2] + (shape[-2] // 2, 2, shape[-1]))
    return ((pairs[..., 0, :] + pairs[..., 1, :]) * 0.5).astype(jnp.bfloat16)


def grouped(per_token, groups):
    return jnp.transpose(per_token.reshape(groups, -1, per_token.shape[-1]), (0, 2, 1))


def ungrouped(blocks):
    return jnp.transpose(blocks, (0, 2, 1)).reshape(-1, blocks.shape[1])


def level_scores(level, query_blocks, key_blocks):
    scale = 1.0 / math.sqrt(HEAD_DIM)
    scores = jnp.einsum(
        "gqhd,gkhd->ghqk", query_blocks, key_blocks, preferred_element_type=jnp.float32
    )
    return jnp.repeat(scores * scale + level * LOG_TWO, 2**level, axis=2)


def body(queries, keys, values, grad_out, w_out):
    seq_devices = lax.axis_size("seq")
    cross = seq_devices.bit_length() - 1
    levels = LOCAL_LEVELS + cross
    position = lax.axis_index("seq")
    scale = 1.0 / math.sqrt(HEAD_DIM)
    query_tok = queries[0]
    key_tok = keys[0]
    value_tok = values[0]
    grad_tok = grad_out[0]
    tokens = query_tok.shape[0]
    width = query_tok.shape[1]
    block = BLOCK
    query_pyramid = [query_tok]
    for level in range(1, levels):
        query_pyramid.append(pooled(query_pyramid[-1]))
    pair_pyramid = [jnp.stack([key_tok, value_tok])]
    level = 1
    pair_pyramid.append(pooled(pair_pyramid[-1]))
    summary = pair_pyramid[LOCAL_LEVELS]
    partners = []
    everyone = lax.all_gather(summary[None], "seq", axis=0, tiled=True)
    for bit in range(cross):
        start = (position >> bit ^ 1) << bit
        members = lax.dynamic_slice_in_dim(everyone, start, 2**bit, 0)
        members = jnp.transpose(members, (1, 0, 2, 3)).reshape(2, 2**bit * block, width)
        for repeat_number in range(bit):
            members = pooled(members)
        partners.append(members)

    def blocks_at(level):
        if level == 0:
            shape = (tokens // (2 * block), 2 * block, HEADS, HEAD_DIM)
            return (query_tok.reshape(shape), key_tok.reshape(shape), value_tok.reshape(shape))
        coarse = query_pyramid[level]
        remote = partners[level - LOCAL_LEVELS]
        shape = (1, block, HEADS, HEAD_DIM)
        return (
            coarse.reshape(1, coarse.shape[0], HEADS, HEAD_DIM),
            remote[0].reshape(shape),
            remote[1].reshape(shape),
        )

    scores_all = []
    top = None
    for level in range(levels):
        query_blocks, key_blocks, value_blocks = blocks_at(level)
        scores = level_scores(level, query_blocks, key_blocks)
        scores_all.append(scores)
        row_top = ungrouped(jnp.max(scores, axis=3))
        top = row_top if top is None else jnp.maximum(top, row_top)
    numer = jnp.zeros((tokens, HEADS, HEAD_DIM), jnp.float32)
    denom = jnp.zeros((tokens, HEADS), jnp.float32)
    for level in range(levels):
        query_blocks, key_blocks, value_blocks = blocks_at(level)
        groups = scores_all[level].shape[0]
        expo = jnp.exp(scores_all[level] - grouped(top, groups)[..., None])
        term = jnp.einsum(
            "ghrk,gkhd->grhd",
            expo.astype(jnp.bfloat16),
            value_blocks,
            preferred_element_type=jnp.float32,
        )
        numer = numer + term.reshape(tokens, HEADS, HEAD_DIM)
        denom = denom + ungrouped(jnp.sum(expo, axis=3))
    attended = (numer / denom[:, :, None]).reshape(tokens, width).astype(jnp.bfloat16)
    mixed = jnp.dot(attended, w_out, preferred_element_type=jnp.float32).astype(jnp.bfloat16)
    grad_att = jnp.einsum("se,de->sd", grad_tok, w_out, preferred_element_type=jnp.float32).astype(
        jnp.bfloat16
    )
    delta = jnp.einsum(
        "shd,shd->sh",
        grad_att.reshape(tokens, HEADS, HEAD_DIM),
        attended.reshape(tokens, HEADS, HEAD_DIM),
        preferred_element_type=jnp.float32,
    )
    query_grads = [jnp.zeros((tokens // 2**level, width), jnp.float32) for level in range(levels)]
    pair_grads = [
        jnp.zeros((2, tokens // 2**level, width), jnp.float32) for level in range(LOCAL_LEVELS + 1)
    ]
    partner_grads = []
    for level in range(levels):
        query_blocks, key_blocks, value_blocks = blocks_at(level)
        groups = scores_all[level].shape[0]
        prob = (
            jnp.exp(scores_all[level] - grouped(top, groups)[..., None])
            / grouped(denom, groups)[..., None]
        )
        grad_rows = grad_att.reshape(groups, -1, HEADS, HEAD_DIM)
        value_grad = jnp.einsum(
            "ghrk,grhd->gkhd",
            prob.astype(jnp.bfloat16),
            grad_rows,
            preferred_element_type=jnp.float32,
        )
        prob_grad = jnp.einsum(
            "grhd,gkhd->ghrk", grad_rows, value_blocks, preferred_element_type=jnp.float32
        )
        score_grad = prob * (prob_grad - grouped(delta, groups)[..., None])
        summed = (
            score_grad.reshape(groups, HEADS, -1, 2**level, score_grad.shape[3])
            .sum(axis=3)
            .astype(jnp.bfloat16)
        )
        query_grad = (
            jnp.einsum("ghqk,gkhd->gqhd", summed, key_blocks, preferred_element_type=jnp.float32)
            * scale
        )
        key_grad = (
            jnp.einsum("ghqk,gqhd->gkhd", summed, query_blocks, preferred_element_type=jnp.float32)
            * scale
        )
        query_grads[level] = query_grad.reshape(-1, width)
        if level == 0:
            pair_grads[0] = jnp.stack(
                [key_grad.reshape(tokens, width), value_grad.reshape(tokens, width)]
            )
        else:
            partner_grads.append(
                jnp.stack([key_grad.reshape(block, width), value_grad.reshape(block, width)])
            )
    upward = jnp.zeros((2, block, width), jnp.float32)
    for bit in reversed(range(cross)):
        spread = 0.5 * jnp.repeat(upward, 2, axis=1)
        upper = position >> bit & 1 == 1
        own_part = jnp.where(upper, spread[:, block:], spread[:, :block])
        their_part = jnp.where(upper, spread[:, :block], spread[:, block:])
        returned = partner(partner_grads[bit] + their_part, "seq", bit)
        upward = own_part + returned
    pair_grads[LOCAL_LEVELS] = upward
    for level in range(levels - 1, 0, -1):
        query_grads[level - 1] = query_grads[level - 1] + 0.5 * jnp.repeat(
            query_grads[level], 2, axis=0
        )
    level = 1
    pair_grads[level - 1] = pair_grads[level - 1] + 0.5 * jnp.repeat(pair_grads[level], 2, axis=1)
    all_tokens = queries.shape[0] * tokens * lax.axis_size("dp") * seq_devices
    factor = 1.0 / math.sqrt(all_tokens)
    weight_term = (
        jnp.einsum("sd,se->de", attended, grad_tok, preferred_element_type=jnp.float32) * factor
    )
    grad_w_out = lax.psum_scatter(weight_term, ("dp", "seq"), scatter_dimension=0, tiled=True)
    grad_queries = query_grads[0].astype(jnp.bfloat16)[None]
    grad_keys = pair_grads[0][0].astype(jnp.bfloat16)[None]
    grad_values = pair_grads[0][1].astype(jnp.bfloat16)[None]
    return (mixed[None], grad_queries, grad_keys, grad_values, grad_w_out)


def solution(mesh):
    placed = (
        P("dp", "seq", None),
        P("dp", "seq", None),
        P("dp", "seq", None),
        P("dp", "seq", None),
        P(),
    )
    return jax.shard_map(
        body,
        mesh=mesh,
        in_specs=placed,
        out_specs=(
            P("dp", "seq", None),
            P("dp", "seq", None),
            P("dp", "seq", None),
            P("dp", "seq", None),
            P(("dp", "seq"), None),
        ),
        check_vma=False,
    )
```

profile of v0, /device:TPU:0, one launch (start us, length us, event | category | flops | bytes accessed | tf_op | source)
XLA Modules:
  0.0 987.6 jit_solution(15692257069907862875)
XLA Ops:
  21.8 2.9 convert_reduce_fusion.1
  34.1 2.6 copy.883
  37.4 50.1 %all-gather.3.cloned.1.call-done = bf16[64,128,1,1024]{3,1,2,0:T(8,128)(2,1)} async-done(((bf16[2,128,1,1024]{3,1,2,0:T(8,128)(2,1)}), bf16[64,128,1,1024]{3,1,2,0:T(8,128)(2,1)}) %all-gather.3.cloned.1.call-update) | async-done | bytes 16777232 | tf_op jit(solution)/shard_map/all_gather | solution.py:67
  87.4 3.2 convert_bitcast_fusion.1
  90.7 8.6 copy.750
  99.3 4.2 fusion.5
  116.3 3.2 copy.744
  119.6 14.2 %fusion.11 = bf16[2,256,1,1024]{3,0,2,1:T(2,128)(2,1)S(1)} fusion(f32[2,256,2,1024]{3,0,2,1:T(2,128)S(1)} %bitcast.449), kind=kLoop, calls=%fused_computation.22 | loop fusion | flops 1572864 | bytes 5242880 | tf_op jit(solution)/shard_map/convert_element_type | solution.py:27
  149.7 11.3 %convert_bitcast_fusion = f32[2,16,128,1024]{3,2,0,1:T(8,128)} fusion(bf16[32,2,128,1024]{3,2,1,0:T(8,128)(2,1)} %bitcast.453, s32[]{:T(128)S(6)} %select_n.66), kind=kLoop, calls=%fused_computation | loop fusion | flops 4194304 | bytes 25165828 | tf_op jit(solution)/shard_map/convert_element_type | solution.py:26
  161.1 27.4 %copy.758 = f32[2,16,128,1024]{3,0,2,1:T(2,128)S(1)} copy(f32[2,16,128,1024]{3,2,0,1:T(8,128)} %convert_bitcast_fusion) | data formatting | bytes 33554432 | tf_op jit(solution)/shard_map/convert_element_type | solution.py:26
  188.5 9.3 fusion.1
  197.8 10.4 %bitcast_convert_fusion = f32[2,512,2,1024]{3,0,2,1:T(2,128)} fusion(bf16[2,512,2,1024]{3,0,2,1:T(2,128)(2,1)} %bitcast.448), kind=kLoop, calls=%fused_computation.11 | loop fusion | flops 2097152 | bytes 12582912 | tf_op jit(solution)/shard_map/convert_element_type | solution.py:26
  208.2 5.3 fusion.3
  292.4 2.5 copy.839
  308.5 3.1 fusion.17
  316.6 3.9 convolution_multiply_fusion
  322.8 2.8 collective-permute-done
  338.9 2.6 maximum_add_fusion.1
  344.7 2.5 reduce_sum.142
  354.0 12.3 %collective-permute-done.1 = f32[2,128,1024]{1,2,0:T(8,128)} collective-permute-done((f32[2,128,1024]{1,2,0:T(8,128)}, f32[2,128,1024]{1,2,0:T(8,128)}, u32[]{:S(2)}, u32[]{:S(2)}) %collective-permute-start.1) | collective-permute-done | bytes 1048608 | tf_op jit(solution)/shard_map/ppermute | solution.py:21
  379.6 2.6 maximum_add_fusion.2
  382.2 3.0 collective-permute-start.2
  386.7 2.6 copy.838
  398.6 9.6 collective-permute-done.2
  421.5 2.6 maximum_add_fusion.3
  431.1 3.0 fusion.81
  434.1 14.1 %collective-permute-done.3 = f32[2,128,1024]{1,2,0:T(8,128)} collective-permute-done((f32[2,128,1024]{1,2,0:T(8,128)}, f32[2,128,1024]{1,2,0:T(8,128)}, u32[]{:S(2)}, u32[]{:S(2)}) %collective-permute-start.3) | collective-permute-done | bytes 1048608 | tf_op jit(solution)/shard_map/ppermute | solution.py:21
  466.5 3.0 mul.451
  469.4 2.7 convolution_multiply_fusion.1
  472.1 2.6 copy.833
  484.8 3.7 mul.480
  491.8 488.5 %reduce-scatter.2.cloned.1.call-done = f32[8,1024]{1,0:T(8,128)} async-done(((f32[1024,1024]{1,0:T(8,128)}), f32[8,1024]{1,0:T(8,128)}) %reduce-scatter.2.cloned.1.call-update) | async-done | bytes 32784 | tf_op jit(solution)/shard_map/reduce_scatter | solution.py:187
  (403 shorter events, 251.2 us)
Async XLA Ops:
  7.2 21.6 %copy-start = (bf16[1024,1024]{1,0:T(8,128)(2,1)S(1)}, bf16[1024,1024]{1,0:T(8,128)(2,1)}, u32[]{:S(2)}) copy-start(bf16[1024,1024]{1,0:T(8,128)(2,1)} %param.9) | copy-start | bytes 6291460
  7.2 80.3 %all-gather.3.cloned.1.call-start = ((), (), s32[]{:S(2)}) async-start(), calls=%async_computation.2 | async-start | bytes 17301504 | tf_op jit(solution)/shard_map/all_gather | solution.py:67
  12.1 968.2 %reduce-scatter.2.cloned.1.call-start = ((), (), s32[]{:S(2)}) async-start(), calls=%async_computation.1 | async-start | bytes 4227072 | tf_op jit(solution)/shard_map/reduce_scatter | solution.py:187
  16.2 211.4 %copy-start.33 = (bf16[128,1,1024]{0,2,1:T(8,128)(2,1)}, bf16[128,1,1024]{0,2,1:T(8,128)(2,1)S(1)}, u32[]{:S(2)}) copy-start(bf16[128,1,1024]{0,2,1:T(8,128)(2,1)S(1)} %copy.930) | copy-start | bytes 786436
  20.9 9.7 copy-start.71
  147.1 13.9 %copy-start.30 = (bf16[1,128,1,1024]{1,3,2,0:T(8,128)(2,1)}, bf16[1,128,1,1024]{1,3,2,0:T(8,128)(2,1)S(1)}, u32[]{:S(2)}) copy-start(bf16[1,128,1,1024]{1,3,2,0:T(8,128)(2,1)S(1)} %copy.739) | copy-start | bytes 786436
  223.0 12.1 %copy-start.28 = (bf16[1,128,1,1024]{1,3,2,0:T(8,128)(2,1)}, bf16[1,128,1,1024]{1,3,2,0:T(8,128)(2,1)S(1)}, u32[]{:S(2)}) copy-start(bf16[1,128,1,1024]{1,3,2,0:T(8,128)(2,1)S(1)} %copy.761) | copy-start | bytes 786436
  227.6 16.7 %copy-start.35 = (bf16[1,1,128,1024]{2,3,1,0:T(8,128)(2,1)}, bf16[1,1,128,1024]{2,3,1,0:T(8,128)(2,1)S(1)}, u32[]{:S(2)}) copy-start(bf16[1,1,128,1024]{2,3,1,0:T(8,128)(2,1)S(1)} %copy.731) | copy-start | bytes 786436
  236.7 10.7 %copy-start.50 = (f32[8,32,8]{0,2,1:T(8,128)S(1)}, f32[8,32,8]{0,2,1:T(8,128)}, u32[]{:S(2)}) copy-start(f32[8,32,8]{0,2,1:T(8,128)} %copy-done.49) | copy-start | bytes 24580
  244.3 9.8 copy-start.51
  247.4 6.8 copy-start.48
  261.1 8.8 copy-start.47
  271.5 6.7 copy-start.46
  296.2 6.0 copy-start.64
  298.5 27.1 %collective-permute-start = (f32[2,128,1024]{1,2,0:T(8,128)}, f32[2,128,1024]{1,2,0:T(8,128)}, u32[]{:S(2)}, u32[]{:S(2)}) collective-permute-start(f32[2,128,1024]{1,2,0:T(8,128)} %pad_maximum_fusion), channel_id=1, source_target_pairs={{0,16},{16,0},{1,17},{17,1},{2,18},{18,2},{3,19},{19,3},{4,20},{20... | collective-permute-start | bytes 3145736 | tf_op jit(solution)/shard_map/ppermute | solution.py:21
  302.2 6.3 copy-start.59
  341.5 5.7 copy-start.34
  341.5 24.8 %collective-permute-start.1 = (f32[2,128,1024]{1,2,0:T(8,128)}, f32[2,128,1024]{1,2,0:T(8,128)}, u32[]{:S(2)}, u32[]{:S(2)}) collective-permute-start(f32[2,128,1024]{1,2,0:T(8,128)} %maximum_add_fusion.1), channel_id=1, source_target_pairs={{0,8},{8,0},{1,9},{9,1},{2,10},{10,2},{3,11},{11,3},{4,12},{12,4},... | collective-permute-start | bytes 3145736 | tf_op jit(solution)/shard_map/ppermute | solution.py:21
  344.7 5.8 copy-start.62
  344.7 5.8 copy-start.75
  352.3 14.0 %copy-start.8 = (f32[2,128,1024]{1,2,0:T(8,128)S(1)}, f32[2,128,1024]{1,2,0:T(8,128)}, u32[]{:S(2)}) copy-start(f32[2,128,1024]{1,2,0:T(8,128)} %copy.918) | copy-start | bytes 3145732
  352.3 14.0 %copy-start.9 = (f32[2,128,1024]{1,2,0:T(8,128)S(1)}, f32[2,128,1024]{1,2,0:T(8,128)}, u32[]{:S(2)}) copy-start(f32[2,128,1024]{1,2,0:T(8,128)} %copy.919) | copy-start | bytes 3145732
  382.2 25.9 %collective-permute-start.2 = (f32[2,128,1024]{1,2,0:T(8,128)}, f32[2,128,1024]{1,2,0:T(8,128)}, u32[]{:S(2)}, u32[]{:S(2)}) collective-permute-start(f32[2,128,1024]{1,2,0:T(8,128)} %maximum_add_fusion.2), channel_id=1, source_target_pairs={{0,4},{4,0},{1,5},{5,1},{2,6},{6,2},{3,7},{7,3},{8,12},{12,8},{9,1... | collective-permute-start | bytes 3145736 | tf_op jit(solution)/shard_map/ppermute | solution.py:21
  386.7 6.8 copy-start.31
  389.2 5.9 copy-start.27
  389.2 7.5 copy-start.76
  396.8 11.4 %copy-start.5 = (f32[2,128,1024]{1,2,0:T(8,128)S(1)}, f32[2,128,1024]{1,2,0:T(8,128)}, u32[]{:S(2)}) copy-start(f32[2,128,1024]{1,2,0:T(8,128)} %copy.920) | copy-start | bytes 3145732
  396.8 11.4 %copy-start.6 = (f32[2,128,1024]{1,2,0:T(8,128)S(1)}, f32[2,128,1024]{1,2,0:T(8,128)}, u32[]{:S(2)}) copy-start(f32[2,128,1024]{1,2,0:T(8,128)} %copy.921) | copy-start | bytes 3145732
  424.0 24.2 %collective-permute-start.3 = (f32[2,128,1024]{1,2,0:T(8,128)}, f32[2,128,1024]{1,2,0:T(8,128)}, u32[]{:S(2)}, u32[]{:S(2)}) collective-permute-start(f32[2,128,1024]{1,2,0:T(8,128)} %maximum_add_fusion.3), channel_id=1, source_target_pairs={{0,2},{2,0},{1,3},{3,1},{4,6},{6,4},{5,7},{7,5},{8,10},{10,8},{9,1... | collective-permute-start | bytes 3145736 | tf_op jit(solution)/shard_map/ppermute | solution.py:21
  431.1 17.1 %copy-start.3 = (f32[2,128,1024]{1,2,0:T(8,128)S(1)}, f32[2,128,1024]{1,2,0:T(8,128)}, u32[]{:S(2)}) copy-start(f32[2,128,1024]{1,2,0:T(8,128)} %copy.922) | copy-start | bytes 3145732
  431.1 17.1 %copy-start.4 = (f32[2,128,1024]{1,2,0:T(8,128)S(1)}, f32[2,128,1024]{1,2,0:T(8,128)}, u32[]{:S(2)}) copy-start(f32[2,128,1024]{1,2,0:T(8,128)} %copy.923) | copy-start | bytes 3145732
  461.2 17.5 %collective-permute-start.4 = (f32[2,128,1024]{1,2,0:T(8,128)}, f32[2,128,1024]{1,2,0:T(8,128)}, u32[]{:S(2)}, u32[]{:S(2)}) collective-permute-start(f32[2,128,1024]{1,2,0:T(8,128)} %maximum_add_fusion.4), channel_id=1, source_target_pairs={{0,1},{1,0},{2,3},{3,2},{4,5},{5,4},{6,7},{7,6},{8,9},{9,8},{10,11... | collective-permute-start | bytes 3145736 | tf_op jit(solution)/shard_map/ppermute | solution.py:21
  (63 other events, 183.7 us)
Sparse Core Ops, SparseCore 0:
  12.2 75.1 all-gather.2
  320.7 659.6 reduce-scatter.1
where the time goes:
time: 999 us; the launch traced here: 988 us
  waiting for transfers between devices  578 us (58%)
  local copies, waits for them, and re-layouts  187 us (19%)
  other arithmetic  138 us (14%)
  matrix products  60.7 us (6%)
  between operations  15.8 us (2%)
    reduce_scatter x1, waiting for transfers between devices, body(): lax.psum_scatter(weight_term, ('dp', 'seq'), scatter_dimension=0, tiled=T...  489 us
    all_gather x1, waiting for transfers between devices, body(): everyone = lax.all_gather(summary[None], 'seq', axis=0, tiled=True)  50.1 us
    convert_element_type x16, other arithmetic, pooled(): return ((pairs[..., 0, :] + pairs[..., 1, :]) * 0.5).astype(jnp.bfloat16)  46.9 us
    convert_element_type x9, local copies, waits for them, and re-layouts, pooled(): rows.astype(jnp.float32)  44.6 us
    convert_element_type x14, other arithmetic, pooled(): rows.astype(jnp.float32)  39.4 us
    ppermute x5, waiting for transfers between devices, partner(): return lax.ppermute(block, axis, route)  38.8 us
    unnamed x195, local copies, waits for them, and re-layouts  33 us
  transfers between devices with their start and end apart: 7, of which 6 were waited for; matrix products, arithmetic and copies ran while one was open for 17% of the time, Pallas kernels for 0%

commit v1 on v0

--- a/solution.py
+++ b/solution.py
@@ -64,7 +64,9 @@
     pair_pyramid.append(pooled(pair_pyramid[-1]))
     summary = pair_pyramid[LOCAL_LEVELS]
     partners = []
-    everyone = lax.all_gather(summary[None], "seq", axis=0, tiled=True)
+    everyone = jnp.concatenate(
+        lax.all_to_all(jnp.stack([summary[None]] * lax.axis_size("seq")), "seq", 0, 0), axis=0
+    )
     for bit in range(cross):
         start = (position >> bit ^ 1) << bit
         members = lax.dynamic_slice_in_dim(everyone, start, 2**bit, 0)

time: 999 us -> 1150 us (1.15)
  waiting for transfers between devices: 578 us -> 687 us
  local copies, waits for them, and re-layouts: 187 us -> 213 us
  starting transfers between devices: 8.49 us -> 28.8 us
    all_to_all x0 -> x1, waiting for transfers between devices: none -> 186 us  [body(): lax.all_to_all(jnp.stack([summary[None]] * lax.axis_size('seq')), 'seq',...]
    all_gather x1 -> x0, waiting for transfers between devices: 50.1 us -> none  [body(): everyone = lax.all_gather(summary[None], 'seq', axis=0, tiled=True)]
    ppermute x5, waiting for transfers between devices: 38.8 us -> 19.7 us  [partner(): return lax.ppermute(block, axis, route)]
    slice x2 -> x9, local copies, waits for them, and re-layouts: 2.68 us -> 17.2 us  [blocks_at(): remote[1].reshape(shape)]
    ppermute x5, starting transfers between devices: 8.41 us -> 20 us  [partner(): return lax.ppermute(block, axis, route)]
    unnamed x195 -> x165, local copies, waits for them, and re-layouts: 33 us -> 23.5 us
  transfers between devices with their start and end apart: 7 -> 7, of which waited for: 6 -> 5; matrix products, arithmetic and copies ran while one was open for 17% -> 15% of each run, Pallas kernels for 0% -> 0%
where the time goes in v1:
time: 1150 us; the launch traced here: 1140 us
  waiting for transfers between devices  687 us (60%)
  local copies, waits for them, and re-layouts  213 us (19%)
  other arithmetic  140 us (12%)
  matrix products  57 us (5%)
  starting transfers between devices  28.8 us (3%)
  between operations  15.6 us (1%)
    reduce_scatter x1, waiting for transfers between devices, body(): lax.psum_scatter(weight_term, ('dp', 'seq'), scatter_dimension=0, tiled=T...  481 us
    all_to_all x1, waiting for transfers between devices, body(): lax.all_to_all(jnp.stack([summary[None]] * lax.axis_size('seq')), 'seq',...  186 us
    convert_element_type x9, local copies, waits for them, and re-layouts, pooled(): rows.astype(jnp.float32)  54.7 us
    convert_element_type x14, other arithmetic, pooled(): rows.astype(jnp.float32)  45.4 us
    convert_element_type x16, other arithmetic, pooled(): return ((pairs[..., 0, :] + pairs[..., 1, :]) * 0.5).astype(jnp.bfloat16)  43.2 us
    unnamed x165, local copies, waits for them, and re-layouts  23.5 us
  transfers between devices with their start and end apart: 7, of which 5 were waited for; matrix products, arithmetic and copies ran while one was open for 15% of the time, Pallas kernels for 0%

profile of v1, /device:TPU:0, one launch (start us, length us, event | category | flops | bytes accessed | tf_op | source)
XLA Modules:
  0.0 1140.8 jit_solution(9968188339966867177)
XLA Ops:
  14.6 7.0 stack.31
  21.6 8.5 all-to-all-start
  32.2 2.9 reshape.1087
  50.1 2.9 convert_reduce_fusion.1
  57.3 186.1 %all-to-all-done = bf16[32,1,2,128,1024]{3,4,2,1,0:T(8,128)(2,1)} async-done(((bf16[32,1,2,128,1024]{3,4,2,1,0:T(8,128)(2,1)}), bf16[32,1,2,128,1024]{3,4,2,1,0:T(8,128)(2,1)}, u32[]{:S(2)}, u32[]{:S(2)}) %all-to-all-start) | async-done | bytes 16777248 | tf_op jit(solution)/shard_map/all_to_all | solution.py:68
  247.0 2.7 convert_bitcast_fusion.3
  249.7 4.7 copy.584
  263.7 3.8 convert_bitcast_fusion.2
  267.5 7.4 copy.592
  274.9 2.9 fusion.11
  286.7 11.1 convert_bitcast_fusion
  297.8 25.1 %copy.606 = f32[2,16,128,1024]{3,0,2,1:T(2,128)} copy(f32[2,16,128,1024]{2,3,0,1:T(8,128)} %convert_bitcast_fusion) | data formatting | bytes 33554432 | tf_op jit(solution)/shard_map/convert_element_type | solution.py:26
  322.9 9.3 fusion.1
  332.2 6.3 convert_bitcast_fusion.1
  338.5 13.2 %copy.598 = f32[2,8,128,1024]{3,0,2,1:T(2,128)} copy(f32[2,8,128,1024]{2,3,0,1:T(8,128)} %convert_bitcast_fusion.1) | data formatting | bytes 16777216 | tf_op jit(solution)/shard_map/convert_element_type | solution.py:26
  351.7 5.5 fusion.5
  370.5 10.4 bitcast_convert_fusion
  380.8 5.5 fusion.3
  471.3 2.7 convolution_multiply_fusion
  474.0 3.2 fusion.17
  482.3 4.6 collective-permute-done
  508.4 8.4 collective-permute-done.1
  531.4 16.9 %collective-permute-start.2 = (f32[2,128,1024]{1,2,0:T(8,128)}, f32[2,128,1024]{1,2,0:T(8,128)}, u32[]{:S(2)}, u32[]{:S(2)}) collective-permute-start(f32[2,128,1024]{1,2,0:T(8,128)} %maximum_add_fusion.2), channel_id=1, source_target_pairs={{0,4},{4,0},{1,5},{5,1},{2,6},{6,2},{3,7},{7,3},{8,12},{12,8},{9,1... | collective-permute-start | bytes 3145736 | tf_op jit(solution)/shard_map/ppermute | solution.py:21
  568.3 3.0 fusion.83
  584.7 2.8 maximum_add_fusion.3
  599.0 2.9 mul.449
  602.0 3.0 fusion.81
  606.7 6.7 collective-permute-done.3
  630.4 2.8 convolution_multiply_fusion.2
  635.8 2.7 fusion.23
  645.5 3.8 mul.478
  652.5 481.2 %reduce-scatter.2.cloned.1.call-done = f32[8,1024]{1,0:T(8,128)} async-done(((f32[1024,1024]{1,0:T(8,128)}), f32[8,1024]{1,0:T(8,128)}) %reduce-scatter.2.cloned.1.call-update) | async-done | bytes 32784 | tf_op jit(solution)/shard_map/reduce_scatter | solution.py:189
  (378 shorter events, 265.2 us)
Async XLA Ops:
  7.2 37.1 %copy-start = (bf16[1024,1024]{1,0:T(8,128)(2,1)S(1)}, bf16[1024,1024]{1,0:T(8,128)(2,1)}, u32[]{:S(2)}) copy-start(bf16[1024,1024]{1,0:T(8,128)(2,1)} %param.9) | copy-start | bytes 6291460
  21.6 8.9 copy-start.39
  21.6 221.8 %all-to-all-start = ((bf16[32,1,2,128,1024]{3,4,2,1,0:T(8,128)(2,1)}), bf16[32,1,2,128,1024]{3,4,2,1,0:T(8,128)(2,1)}, u32[]{:S(2)}, u32[]{:S(2)}) async-start(bf16[32,1,2,128,1024]{3,4,2,1,0:T(8,128)(2,1)} %stack.31), calls=%async_computation | async-start | bytes 33554432 | tf_op jit(solution)/shard_map/all_to_all | solution.py:68
  30.1 1103.5 %reduce-scatter.2.cloned.1.call-start = ((), (), s32[]{:S(2)}) async-start(), calls=%async_computation.2 | async-start | bytes 4227072 | tf_op jit(solution)/shard_map/reduce_scatter | solution.py:189
  30.7 8.9 copy-start.13
  32.2 7.5 copy-start.12
  50.1 195.1 %copy-start.33 = (bf16[128,1,1024]{0,2,1:T(8,128)(2,1)S(1)}, bf16[128,1,1024]{0,2,1:T(8,128)(2,1)}, u32[]{:S(2)}) copy-start(bf16[128,1,1024]{0,2,1:T(8,128)(2,1)} %copy.782) | copy-start | bytes 786436
  261.1 6.5 copy-start.24
  284.2 13.5 %copy-start.22 = (bf16[1,128,1,1024]{1,3,2,0:T(8,128)(2,1)}, bf16[1,128,1,1024]{1,3,2,0:T(8,128)(2,1)S(1)}, u32[]{:S(2)}) copy-start(bf16[1,128,1,1024]{1,3,2,0:T(8,128)(2,1)S(1)} %copy.595) | copy-start | bytes 786436
  368.2 12.7 %copy-start.26 = (bf16[1,128,1,1024]{1,3,2,0:T(8,128)(2,1)}, bf16[1,128,1,1024]{1,3,2,0:T(8,128)(2,1)S(1)}, u32[]{:S(2)}) copy-start(bf16[1,128,1,1024]{1,3,2,0:T(8,128)(2,1)S(1)} %copy.601) | copy-start | bytes 786436
  397.3 15.9 %copy-start.28 = (bf16[1,128,1,1024]{1,3,2,0:T(8,128)(2,1)}, bf16[1,128,1,1024]{1,3,2,0:T(8,128)(2,1)S(1)}, u32[]{:S(2)}) copy-start(bf16[1,128,1,1024]{1,3,2,0:T(8,128)(2,1)S(1)} %copy.609) | copy-start | bytes 786436
  401.4 14.5 %copy-start.42 = (f32[8,16,16]{0,2,1:T(8,128)}, f32[8,16,16]{0,2,1:T(8,128)S(1)}, u32[]{:S(2)}) copy-start(f32[8,16,16]{0,2,1:T(8,128)S(1)} %reduce_max.175) | copy-start | bytes 24580
  423.9 10.0 copy-start.59
  423.9 10.1 copy-start.55
  423.9 13.2 %copy-start.52 = (f32[8,128]{0,1:T(8,128)S(1)}, f32[8,128]{0,1:T(8,128)}, u32[]{:S(2)}) copy-start(f32[8,128]{0,1:T(8,128)} %copy.582) | copy-start | bytes 12292
  447.0 7.0 copy-start.64
  447.6 9.3 copy-start.11
  470.2 16.6 %collective-permute-start = (f32[2,128,1024]{1,2,0:T(8,128)}, f32[2,128,1024]{1,2,0:T(8,128)}, u32[]{:S(2)}, u32[]{:S(2)}) collective-permute-start(f32[2,128,1024]{1,2,0:T(8,128)} %pad_maximum_fusion), channel_id=1, source_target_pairs={{0,16},{16,0},{1,17},{17,1},{2,18},{18,2},{3,19},{19,3},{4,20},{20... | collective-permute-start | bytes 3145736 | tf_op jit(solution)/shard_map/ppermute | solution.py:21
  501.9 14.9 %collective-permute-start.1 = (f32[2,128,1024]{1,2,0:T(8,128)S(1)}, f32[2,128,1024]{1,2,0:T(8,128)S(1)}, u32[]{:S(2)}, u32[]{:S(2)}) collective-permute-start(f32[2,128,1024]{1,2,0:T(8,128)S(1)} %maximum_add_fusion.1), channel_id=1, source_target_pairs={{0,8},{8,0},{1,9},{9,1},{2,10},{10,2},{3,11},{11,3},{4,12},{12,4},... | collective-permute-start | bytes 3145736 | tf_op jit(solution)/shard_map/ppermute | solution.py:21
  506.8 10.0 copy-start.9
  506.8 10.0 copy-start.10
  528.8 19.4 %copy-start.23 = (bf16[1,128,1,1024]{1,3,2,0:T(8,128)(2,1)S(1)}, bf16[1,128,1,1024]{1,3,2,0:T(8,128)(2,1)}, u32[]{:S(2)}) copy-start(bf16[1,128,1,1024]{1,3,2,0:T(8,128)(2,1)} %copy-done.22) | copy-start | bytes 786436
  528.8 19.4 %copy-start.58 = (bf16[8,32,128]{2,1,0:T(8,128)(2,1)S(1)}, bf16[8,32,128]{2,1,0:T(8,128)(2,1)}, u32[]{:S(2)}) copy-start(bf16[8,32,128]{2,1,0:T(8,128)(2,1)} %copy-done.57) | copy-start | bytes 196612
  531.4 22.3 %copy-start.47 = (f32[1,64,8,128]{3,1,2,0:T(8,128)S(1)}, f32[1,64,8,128]{3,1,2,0:T(8,128)}, u32[]{:S(2)}) copy-start(f32[1,64,8,128]{3,1,2,0:T(8,128)} %fusion.32) | copy-start | bytes 786436
  531.4 40.0 %collective-permute-start.2 = (f32[2,128,1024]{1,2,0:T(8,128)}, f32[2,128,1024]{1,2,0:T(8,128)}, u32[]{:S(2)}, u32[]{:S(2)}) collective-permute-start(f32[2,128,1024]{1,2,0:T(8,128)} %maximum_add_fusion.2), channel_id=1, source_target_pairs={{0,4},{4,0},{1,5},{5,1},{2,6},{6,2},{3,7},{7,3},{8,12},{12,8},{9,1... | collective-permute-start | bytes 3145736 | tf_op jit(solution)/shard_map/ppermute | solution.py:21
  554.8 7.2 copy-start.41
  557.8 7.4 copy-start.31
  587.5 8.1 copy-start.68
  587.5 25.9 %collective-permute-start.3 = (f32[2,128,1024]{1,2,0:T(8,128)}, f32[2,128,1024]{1,2,0:T(8,128)}, u32[]{:S(2)}, u32[]{:S(2)}) collective-permute-start(f32[2,128,1024]{1,2,0:T(8,128)} %maximum_add_fusion.3), channel_id=1, source_target_pairs={{0,2},{2,0},{1,3},{3,1},{4,6},{6,4},{5,7},{7,5},{8,10},{10,8},{9,1... | collective-permute-start | bytes 3145736 | tf_op jit(solution)/shard_map/ppermute | solution.py:21
  605.0 8.4 copy-start.6
  605.0 8.4 copy-start.7
  626.5 12.9 %collective-permute-start.4 = (f32[2,128,1024]{1,2,0:T(8,128)}, f32[2,128,1024]{1,2,0:T(8,128)}, u32[]{:S(2)}, u32[]{:S(2)}) collective-permute-start(f32[2,128,1024]{1,2,0:T(8,128)} %maximum_add_fusion.4), channel_id=1, source_target_pairs={{0,1},{1,0},{2,3},{3,2},{4,5},{5,4},{6,7},{7,6},{8,9},{9,8},{10,11... | collective-permute-start | bytes 3145736 | tf_op jit(solution)/shard_map/ppermute | solution.py:21
  (52 other events, 133.5 us)
Sparse Core Ops, SparseCore 0:
  474.1 659.4 reduce-scatter.1
